TPU v7x, 32 devices: a whole 2x2x4 slice. The times are simulated.
32 devices in a mesh: fsdp: 4 (over y, core), ctx: 2 (over x), tp: 4 (over z).
Axes of the slice: x: 2, y: 2, z: 4, core: 2. Of those that a mesh axis runs over, the one named last changes fastest.
Arguments:
- tokens: bfloat16 [4, 1024, 2048], P('fsdp', 'ctx'), may hold values from -6 to 6
- lengths: int32 [4, 3], P('fsdp'), may hold values from 1 to 768, 960 in all within a row
- block_order: int32 [4, 4], P('fsdp'), may hold values from 0 to 3, each once within a row
- ln_gain: bfloat16 [2048], P('fsdp'), may hold values from 0.25 to 1.75
- ln_bias: bfloat16 [2048], P('fsdp'), may hold values from -3 to 3
- qkv_weight: bfloat16 [2048, 3, 2048], P('fsdp', None, 'tp'), may hold values from -0.125 to 0.125
- qkv_bias: bfloat16 [3, 2048], P(None, 'tp'), may hold values from -0.59765625 to 0.59765625
- dense_weight: bfloat16 [2048, 2048], P('fsdp', 'tp'), may hold values from -1 to 1
- dense_bias: bfloat16 [2048], P('fsdp'), may hold values from -3 to 3
- fc1_weight: bfloat16 [2048, 8192], P('fsdp', 'tp'), may hold values from -0.125 to 0.125
- fc1_bias: bfloat16 [8192], P('tp'), may hold values from -3 to 3
- fc2_weight: bfloat16 [2048, 8192], P('fsdp', 'tp'), may hold values from -0.0625 to 0.0625
- fc2_bias: bfloat16 [2048], P('fsdp'), may hold values from -3 to 3
- cotangent: bfloat16 [4, 1024, 2048], P('fsdp', 'ctx'), may hold values from -6 to 6
Outputs:
- output: bfloat16 [4, 1024, 2048], P('fsdp', 'ctx')
- input_grad: float32 [4, 1024, 2048], P('fsdp', 'ctx')
- ln_gain_grad: float32 [2048], P('fsdp')
- ln_bias_grad: float32 [2048], P('fsdp')
- qkv_weight_grad: float32 [2048, 3, 2048], P('fsdp', None, 'tp')
- qkv_bias_grad: float32 [3, 2048], P(None, 'tp')
- dense_weight_grad: float32 [2048, 2048], P('fsdp', 'tp')
- dense_bias_grad: float32 [2048], P('fsdp')
- fc1_weight_grad: float32 [2048, 8192], P('fsdp', 'tp')
- fc1_bias_grad: float32 [8192], P('tp')
- fc2_weight_grad: float32 [2048, 8192], P('fsdp', 'tp')
- fc2_bias_grad: float32 [2048], P('fsdp')
Inputs may be any that keep to these rules, and one draw needn't show every extreme that they name: Each row holds the lengths of 3 sequences packed from the row's start; they sum to 960 and the largest is exactly 768. Each row is a permutation of the 4 block numbers; dealt block j holds packed block block_order[b, j].
All inputs are finite; a program needn't handle non-finite values.
Results may differ from a plain program's by a relative error of at most 0.012.
Values may be sent and summed in bfloat16 or wider, within the bound.
No kernel may reach another device: no remote copies, remote signals or barrier semaphores. Data moves between devices by JAX's collectives and lax.ppermute only.
A program may use at most 256 MiB of HBM per device.

v0:
```python
import math
import jax
import jax.numpy as jnp
from jax import lax
from jax.sharding import PartitionSpec as P

HD = 256
ROT = 64
NORM_EPSILON = 1e-05
MASK_FLOOR = -1000000000.0


def rotation_tables(position):
    frequency = jnp.exp(jnp.arange(ROT // 2, dtype=jnp.float32) * (-2.0 * math.log(10000.0) / ROT))
    angles = position.astype(jnp.float32)[:, None] * frequency[None, :]
    return (jnp.cos(angles)[:, None, :], jnp.sin(angles)[:, None, :])


def rotate(values, cosine_table, sine_table):
    first_half = values[..., : ROT // 2]
    second_half = values[..., ROT // 2 : ROT]
    return jnp.concatenate(
        [
            first_half * cosine_table - second_half * sine_table,
            second_half * cosine_table + first_half * sine_table,
            values[..., ROT:],
        ],
        axis=-1,
    )


def rotate_back(grads, cosine_table, sine_table):
    first_half = grads[..., : ROT // 2]
    second_half = grads[..., ROT // 2 : ROT]
    return jnp.concatenate(
        [
            first_half * cosine_table + second_half * sine_table,
            second_half * cosine_table - first_half * sine_table,
            grads[..., ROT:],
        ],
        axis=-1,
    )


def packed_rows(order_row, first_slot, row_count, block_rows):
    row_index = jnp.arange(row_count, dtype=jnp.int32)
    dealt_slot = first_slot + row_index // block_rows
    selector = dealt_slot[:, None] == jnp.arange(order_row.shape[0], dtype=jnp.int32)[None, :]
    source_block = jnp.sum(jnp.where(selector, order_row[None, :], 0), axis=1, dtype=jnp.int32)
    return source_block * block_rows + row_index % block_rows


def place_rows(packed_at, lengths_row):
    seq_ends = jnp.cumsum(lengths_row, dtype=jnp.int32)
    passed = packed_at[:, None] >= seq_ends[None, :]
    segment = jnp.sum(passed.astype(jnp.int32), axis=1, dtype=jnp.int32)
    before = jnp.sum(jnp.where(passed, lengths_row[None, :], 0), axis=1, dtype=jnp.int32)
    return (segment, packed_at - before)


def gelu_slope(value):
    normal_cdf = 0.5 * (1.0 + lax.erf(value * (1.0 / math.sqrt(2.0))))
    density = jnp.exp(-0.5 * value * value) * (1.0 / math.sqrt(2.0 * math.pi))
    return normal_cdf + value * density


def per_device(
    tokens,
    lengths,
    block_order,
    ln_gain,
    ln_bias,
    qkv_weight,
    qkv_bias,
    dense_weight,
    dense_bias,
    fc1_weight,
    fc1_bias,
    fc2_weight,
    fc2_bias,
    cotangent,
):
    gathered = (
        lax.all_gather(qkv_weight, "fsdp", axis=0, tiled=True),
        lax.all_gather(dense_weight, "fsdp", axis=0, tiled=True),
        lax.all_gather(fc1_weight, "fsdp", axis=0, tiled=True),
        lax.all_gather(fc2_weight, "fsdp", axis=0, tiled=True),
        lax.all_gather(ln_gain, "fsdp", axis=0, tiled=True),
        lax.all_gather(ln_bias, "fsdp", axis=0, tiled=True),
        lax.all_gather(dense_bias, "fsdp", axis=0, tiled=True),
        lax.all_gather(fc2_bias, "fsdp", axis=0, tiled=True),
    )
    qkv_full = gathered[0]
    dense_full = gathered[1]
    fc1_full = gathered[2]
    fc2_full = gathered[3]
    norm_gain = gathered[4].astype(jnp.float32)
    norm_bias = gathered[5].astype(jnp.float32)
    out_bias = gathered[6].astype(jnp.float32) + gathered[7].astype(jnp.float32)
    inputs = tokens[0].astype(jnp.float32)
    row_count = inputs.shape[0]
    block_rows = row_count // 2
    group_rows = row_count * lax.axis_size("ctx")
    lengths_row = lengths[0]
    order_row = block_order[0]
    seq_count = lengths_row.shape[0]
    local_packed = packed_rows(order_row, lax.axis_index("ctx") * 2, row_count, block_rows)
    key_packed = packed_rows(order_row, 0, group_rows, block_rows)
    local_segment, local_position = place_rows(local_packed, lengths_row)
    key_segment = place_rows(key_packed, lengths_row)[0]
    valid_rows = (local_segment < seq_count).astype(jnp.float32)
    allowed = (local_segment[:, None] == key_segment[None, :]) & (
        key_packed[None, :] <= local_packed[:, None]
    )
    cosine_table, sine_table = rotation_tables(local_position)
    score_scale = 1.0 / math.sqrt(HD)
    row_mean = jnp.mean(inputs, axis=1, keepdims=True)
    centred = inputs - row_mean
    variance = jnp.mean(centred * centred, axis=1, keepdims=True)
    inverse = lax.rsqrt(variance + NORM_EPSILON)
    standard = centred * inverse
    normed = (standard * norm_gain + norm_bias).astype(jnp.bfloat16)
    projected = jnp.einsum(
        "td,dce->tce", normed, qkv_full, preferred_element_type=jnp.float32
    ) + qkv_bias.astype(jnp.float32)
    heads_here = projected.shape[2] // HD
    shaped = projected.reshape(row_count, 3, heads_here, HD)
    queries = rotate(shaped[:, 0], cosine_table, sine_table).astype(jnp.bfloat16)
    keys_local = rotate(shaped[:, 1], cosine_table, sine_table).astype(jnp.bfloat16)
    values_local = shaped[:, 2].astype(jnp.bfloat16)
    keys_all, values_all = (
        lax.all_gather(keys_local, "ctx", axis=0, tiled=True),
        lax.all_gather(values_local, "ctx", axis=0, tiled=True),
    )

    def head_scores(head_index):
        scores = (
            jnp.einsum(
                "qe,ke->qk",
                queries[:, head_index],
                keys_all[:, head_index],
                preferred_element_type=jnp.float32,
            )
            * score_scale
        )
        return jnp.where(allowed, scores, MASK_FLOOR)

    head_outputs = []
    log_totals = []
    for head_index in range(heads_here):
        scores = head_scores(head_index)
        row_max = jnp.max(scores, axis=1, keepdims=True)
        exp_scores = jnp.exp(scores - row_max)
        row_total = jnp.sum(exp_scores, axis=1, keepdims=True)
        probabilities = (exp_scores / row_total).astype(jnp.bfloat16)
        head_outputs.append(
            jnp.dot(probabilities, values_all[:, head_index], preferred_element_type=jnp.float32)
        )
        log_totals.append(row_max + jnp.log(row_total))
    attended = (
        (jnp.stack(head_outputs, axis=1) * valid_rows[:, None, None])
        .astype(jnp.bfloat16)
        .reshape(row_count, heads_here * HD)
    )
    pre_act = jnp.dot(normed, fc1_full, preferred_element_type=jnp.float32) + fc1_bias.astype(
        jnp.float32
    )
    hidden = jax.nn.gelu(pre_act, approximate=False).astype(jnp.bfloat16)
    partial_out = jnp.einsum(
        "te,de->td", attended, dense_full, preferred_element_type=jnp.float32
    ) + jnp.einsum("tf,df->td", hidden, fc2_full, preferred_element_type=jnp.float32)
    summed = lax.psum(partial_out, "tp")
    output = (inputs + summed + out_bias).astype(jnp.bfloat16)
    upstream_low = cotangent[0]
    upstream = upstream_low.astype(jnp.float32)
    out_bias_grad = jnp.sum(upstream, axis=0)
    dense_grad = jnp.einsum("td,te->de", upstream_low, attended, preferred_element_type=jnp.float32)
    fc2_grad = jnp.einsum("td,tf->df", upstream_low, hidden, preferred_element_type=jnp.float32)
    attended_grad = (
        jnp.dot(upstream_low, dense_full, preferred_element_type=jnp.float32).astype(jnp.bfloat16)
        * valid_rows[:, None].astype(jnp.bfloat16)
    ).reshape(row_count, heads_here, HD)
    hidden_grad = jnp.dot(upstream_low, fc2_full, preferred_element_type=jnp.float32)
    pre_grad = (hidden_grad * gelu_slope(pre_act)).astype(jnp.bfloat16)
    fc1_bias_grad = jnp.sum(pre_grad.astype(jnp.float32), axis=0)
    fc1_grad = jnp.einsum("td,tf->df", normed, pre_grad, preferred_element_type=jnp.float32)
    normed_grad = jnp.einsum("tf,df->td", pre_grad, fc1_full, preferred_element_type=jnp.float32)
    query_pieces = []
    key_pieces = []
    value_pieces = []
    for head_index in range(heads_here):
        probs_full = jnp.exp(head_scores(head_index) - log_totals[head_index])
        probs_low = probs_full.astype(jnp.bfloat16)
        head_grad = attended_grad[:, head_index]
        prob_grad = jnp.einsum(
            "qe,ke->qk", head_grad, values_all[:, head_index], preferred_element_type=jnp.float32
        )
        row_delta = jnp.sum(probs_full * prob_grad, axis=1, keepdims=True)
        score_grad = (probs_full * (prob_grad - row_delta)).astype(jnp.bfloat16)
        query_pieces.append(
            jnp.dot(score_grad, keys_all[:, head_index], preferred_element_type=jnp.float32)
            * score_scale
        )
        key_pieces.append(
            jnp.einsum(
                "qk,qe->ke", score_grad, queries[:, head_index], preferred_element_type=jnp.float32
            )
            * score_scale
        )
        value_pieces.append(
            jnp.einsum("qk,qe->ke", probs_low, head_grad, preferred_element_type=jnp.float32)
        )
    own_keys, own_values = (
        lax.psum_scatter(jnp.stack(key_pieces, axis=1), "ctx", scatter_dimension=0, tiled=True),
        lax.psum_scatter(jnp.stack(value_pieces, axis=1), "ctx", scatter_dimension=0, tiled=True),
    )
    query_turned = rotate_back(jnp.stack(query_pieces, axis=1), cosine_table, sine_table)
    key_turned = rotate_back(own_keys, cosine_table, sine_table)
    proj_grad = (
        jnp.stack([query_turned, key_turned, own_values], axis=1)
        .astype(jnp.bfloat16)
        .reshape(row_count, 3, heads_here * HD)
    )
    qkv_bias_grad = jnp.sum(proj_grad.astype(jnp.float32), axis=0)
    qkv_grad = jnp.einsum("td,tce->dce", normed, proj_grad, preferred_element_type=jnp.float32)
    normed_grad = normed_grad + jnp.einsum(
        "tce,dce->td", proj_grad, qkv_full, preferred_element_type=jnp.float32
    )
    full_grad = lax.psum(normed_grad, "tp")
    gain_grad = jnp.sum(full_grad * standard, axis=0)
    shift_grad = jnp.sum(full_grad, axis=0)
    scaled = full_grad * norm_gain
    input_grad = upstream + inverse * (
        scaled
        - jnp.mean(scaled, axis=1, keepdims=True)
        - standard * jnp.mean(scaled * standard, axis=1, keepdims=True)
    )
    bias_sums = lax.psum((qkv_bias_grad, fc1_bias_grad), ("fsdp", "ctx"))
    reduced = (
        lax.psum_scatter(qkv_grad, ("fsdp", "ctx"), scatter_dimension=0, tiled=True),
        lax.psum_scatter(dense_grad, ("fsdp", "ctx"), scatter_dimension=0, tiled=True),
        lax.psum_scatter(fc1_grad, ("fsdp", "ctx"), scatter_dimension=0, tiled=True),
        lax.psum_scatter(fc2_grad, ("fsdp", "ctx"), scatter_dimension=0, tiled=True),
        lax.psum_scatter(gain_grad, ("fsdp", "ctx"), scatter_dimension=0, tiled=True),
        lax.psum_scatter(shift_grad, ("fsdp", "ctx"), scatter_dimension=0, tiled=True),
        lax.psum_scatter(out_bias_grad, ("fsdp", "ctx"), scatter_dimension=0, tiled=True),
    )
    shards = (
        lax.all_gather(reduced[0], "ctx", axis=0, tiled=True),
        lax.all_gather(reduced[1], "ctx", axis=0, tiled=True),
        lax.all_gather(reduced[2], "ctx", axis=0, tiled=True),
        lax.all_gather(reduced[3], "ctx", axis=0, tiled=True),
        lax.all_gather(reduced[4], "ctx", axis=0, tiled=True),
        lax.all_gather(reduced[5], "ctx", axis=0, tiled=True),
        lax.all_gather(reduced[6], "ctx", axis=0, tiled=True),
    )
    return (
        output[None],
        input_grad[None],
        shards[4],
        shards[5],
        shards[0],
        bias_sums[0],
        shards[1],
        shards[6],
        shards[2],
        bias_sums[1],
        shards[3],
        shards[6],
    )


def solution(mesh):
    placed = (
        P("fsdp", "ctx", None),
        P("fsdp", None),
        P("fsdp", None),
        P("fsdp"),
        P("fsdp"),
        P("fsdp", None, "tp"),
        P(None, "tp"),
        P("fsdp", "tp"),
        P("fsdp"),
        P("fsdp", "tp"),
        P("tp"),
        P("fsdp", "tp"),
        P("fsdp"),
        P("fsdp", "ctx", None),
    )
    return jax.shard_map(
        per_device,
        mesh=mesh,
        in_specs=placed,
        out_specs=(
            P("fsdp", "ctx", None),
            P("fsdp", "ctx", None),
            P("fsdp"),
            P("fsdp"),
            P("fsdp", None, "tp"),
            P(None, "tp"),
            P("fsdp", "tp"),
            P("fsdp"),
            P("fsdp", "tp"),
            P("tp"),
            P("fsdp", "tp"),
            P("fsdp"),
        ),
        check_vma=False,
    )
```

profile of v0, /device:TPU:0, one launch (start us, length us, event | category | flops | bytes accessed | tf_op | source)
XLA Modules:
  0.0 1210.0 jit_solution(16124537954326559841)
XLA Ops:
  11.0 6.2 all-gather.2
  17.2 5.5 all-gather.1
  24.5 34.9 %all-gather.19.cloned.1.call-done = bf16[2048,3,512]{0,2,1:T(8,128)(2,1)} async-done(((bf16[512,3,512]{0,2,1:T(8,128)(2,1)}), bf16[2048,3,512]{0,2,1:T(8,128)(2,1)}) %all-gather.19.cloned.1.call-update) | async-done | bytes 6291472 | tf_op jit(solution)/shard_map/all_gather | solution.py:84
  59.3 5.9 fusion.46
  69.2 14.3 %all-gather.23.cloned.1.call-done = bf16[2048,512]{1,0:T(8,128)(2,1)} async-done(((bf16[512,512]{1,0:T(8,128)(2,1)}), bf16[2048,512]{1,0:T(8,128)(2,1)}) %all-gather.23.cloned.1.call-update) | async-done | bytes 2097168 | tf_op jit(solution)/shard_map/all_gather | solution.py:85
  90.9 16.0 %all-gather.21.cloned.1.call-done = bf16[1024,2,256]{0,2,1:T(8,128)(2,1)} async-done(((bf16[512,2,256]{0,2,1:T(8,128)(2,1)}), bf16[1024,2,256]{0,2,1:T(8,128)(2,1)}) %all-gather.21.cloned.1.call-update) | async-done | bytes 1048592 | tf_op jit(solution)/shard_map/all_gather | solution.py:132
  114.5 15.7 %all-gather.37.cloned.1.call-done = bf16[1024,1,2,256]{0,3,2,1:T(8,128)(2,1)} async-done(((bf16[512,1,2,256]{0,3,2,1:T(8,128)(2,1)}), bf16[1024,1,2,256]{0,3,2,1:T(8,128)(2,1)}) %all-gather.37.cloned.1.call-update) | async-done | bytes 1048592 | tf_op jit(solution)/shard_map/all_gather | solution.py:133
  152.3 12.5 %reduce-scatter.9.cloned.1.call-done = f32[512,2,256]{2,0,1:T(8,128)} async-done(((f32[1024,2,256]{2,0,1:T(8,128)}), f32[512,2,256]{2,0,1:T(8,128)}) %reduce-scatter.9.cloned.1.call-update) | async-done | bytes 1048592 | tf_op jit(solution)/shard_map/reduce_scatter | solution.py:215
  171.0 28.4 %reduce-scatter.7.cloned.1.call-done = f32[512,2,256]{0,2,1:T(8,128)} async-done(((f32[1024,2,256]{0,2,1:T(8,128)}), f32[512,2,256]{0,2,1:T(8,128)}) %reduce-scatter.7.cloned.1.call-update) | async-done | bytes 1048592 | tf_op jit(solution)/shard_map/reduce_scatter | solution.py:214
  207.2 8.8 fusion.40
  216.7 42.6 %all-gather.25.cloned.1.call-done = bf16[2048,2048]{1,0:T(8,128)(2,1)} async-done(((bf16[512,2048]{1,0:T(8,128)(2,1)}), bf16[2048,2048]{1,0:T(8,128)(2,1)}) %all-gather.25.cloned.1.call-update) | async-done | bytes 8388624 | tf_op jit(solution)/shard_map/all_gather | solution.py:86
  259.3 17.2 %fusion.20 = (bf16[512,2048]{1,0:T(8,128)(2,1)}, f32[512,2048]{1,0:T(8,128)}) fusion(f32[2048]{0:T(1024)S(1)} %convert_element_type.135, bf16[2048,2048]{1,0:T(8,128)(2,1)} %all-gather.25.cloned.1.call-done, bf16[1,512,2048]{2,1,0:T(8,128)(2,1)S(1)} %copy-done, f32[2048]{0:T(1024)S(1)} %bitcast.223, f32[2048]{0:T(1024)S(1)} %bitcast.214, ...), kind=kOutput, calls=%fused_computation.27 | convolution fusion | flops 4370464768 | bytes 16805888 | tf_op jit(solution)/shard_map/dot_general | solution.py:165
  276.5 42.7 %all-gather.27.cloned.1.call-done = bf16[2048,2048]{1,0:T(8,128)(2,1)} async-done(((bf16[512,2048]{1,0:T(8,128)(2,1)}), bf16[2048,2048]{1,0:T(8,128)(2,1)}) %all-gather.27.cloned.1.call-update) | async-done | bytes 8388624 | tf_op jit(solution)/shard_map/all_gather | solution.py:87
  319.2 9.4 convert_reduce_fusion.2
  329.9 8.8 fusion.92
  339.2 12.5 %convolution_bitcast_fusion = f32[2048,2048]{0,1:T(8,128)} fusion(bf16[512,2048]{1,0:T(8,128)(2,1)} %get-tuple-element.96, bf16[1,512,2048]{2,1,0:T(8,128)(2,1)} %param.27), kind=kOutput, calls=%fused_computation | convolution fusion | flops 4294967296 | bytes 20971520 | tf_op jit(solution)/shard_map/td,tf->df/dot_general | solution.py:178
  353.3 10.8 fusion.99
  364.1 9.8 fusion.100
  374.5 6.5 convolution_add_fusion
  381.0 8.7 bitcast_add_fusion
  389.8 79.9 %reduce-scatter.11.cloned.1.call-done = f32[256,3,512]{2,0,1:T(8,128)} async-done(((f32[2048,3,512]{2,0,1:T(8,128)}), f32[256,3,512]{2,0,1:T(8,128)}) %reduce-scatter.11.cloned.1.call-update) | async-done | bytes 1572880 | tf_op jit(solution)/shard_map/reduce_scatter | solution.py:240
  469.7 119.7 %reduce-scatter.15.cloned.1.call-done = f32[256,2048]{1,0:T(8,128)} async-done(((f32[2048,2048]{1,0:T(8,128)}), f32[256,2048]{1,0:T(8,128)}) %reduce-scatter.15.cloned.1.call-update) | async-done | bytes 2097168 | tf_op jit(solution)/shard_map/reduce_scatter | solution.py:242
  589.5 119.4 %reduce-scatter.17.cloned.1.call-done = f32[256,2048]{0,1:T(8,128)} async-done(((f32[2048,2048]{0,1:T(8,128)}), f32[256,2048]{0,1:T(8,128)}) %reduce-scatter.17.cloned.1.call-update) | async-done | bytes 2097168 | tf_op jit(solution)/shard_map/reduce_scatter | solution.py:243
  710.2 5.2 all-gather.4
  715.4 5.2 all-gather.3
  721.9 9.8 all-gather.31.cloned.1.call-done
  734.3 291.4 %all-reduce.7.cloned.1.call-done = (f32[512,2048]{1,0:T(8,128)}, f32[512,2048]{1,0:T(8,128)}) async-done(((f32[512,2048]{1,0:T(8,128)}, f32[512,2048]{1,0:T(8,128)}), (f32[512,2048]{1,0:T(8,128)}, f32[512,2048]{1,0:T(8,128)})) %all-reduce.7.cloned.1.call-update) | async-done | bytes 8388624 | tf_op jit(solution)/shard_map/psum | solution.py:172
  1029.8 6.1 convert_reduce_fusion
  1035.8 28.5 %all-reduce.3 = (f32[2048]{0:T(1024)S(1)}, f32[2048]{0:T(1024)S(1)}, f32[3,512]{1,0:T(4,128)}, f32[2048]{0:T(1024)S(1)}, f32[2048]{0:T(1024)}) all-reduce(f32[2048]{0:T(1024)S(1)} %get-tuple-element.60, f32[2048]{0:T(1024)S(1)} %get-tuple-element.63, ...), channel_id=5, replica_groups=mesh['fsdp'=4,'ctx'=2,'tp'=4] {'fsdp','ctx'}, use_global_device_ids=true, to_apply=%region_21.22.clone | all-reduce | flops 9728 | bytes 77824
  1077.5 54.2 %all-gather.33.cloned.1.call-done = f32[512,2048]{1,0:T(8,128)} async-done(((f32[256,2048]{1,0:T(8,128)}), f32[512,2048]{1,0:T(8,128)}) %all-gather.33.cloned.1.call-update) | async-done | bytes 4194320 | tf_op jit(solution)/shard_map/all_gather | solution.py:251
  1131.6 58.1 %all-gather.35.cloned.1.call-done = f32[512,2048]{0,1:T(8,128)} async-done(((f32[256,2048]{0,1:T(8,128)}), f32[512,2048]{0,1:T(8,128)}) %all-gather.35.cloned.1.call-update) | async-done | bytes 4194320 | tf_op jit(solution)/shard_map/all_gather | solution.py:252
  1189.8 5.3 copy.67
  (207 shorter events, 94.6 us)
Async XLA Ops:
  7.2 15.5 %copy-start.30 = (bf16[3,512]{1,0:T(4,128)(2,1)S(1)}, bf16[3,512]{1,0:T(4,128)(2,1)}, u32[]{:S(2)}) copy-start(bf16[3,512]{1,0:T(4,128)(2,1)} %param.20) | copy-start | bytes 9220
  7.2 15.5 %copy-start.37 = (s32[1,3]{1,0:T(1,128)S(1)}, s32[1,3]{1,0:T(1,128)}, u32[]{:S(2)}) copy-start(s32[1,3]{1,0:T(1,128)} %param.15) | copy-start | bytes 40
  7.2 15.8 %copy-start = (bf16[1,512,2048]{2,1,0:T(8,128)(2,1)S(1)}, bf16[1,512,2048]{2,1,0:T(8,128)(2,1)}, u32[]{:S(2)}) copy-start(bf16[1,512,2048]{2,1,0:T(8,128)(2,1)} %param.14) | copy-start | bytes 6291460
  7.2 52.1 %all-gather.19.cloned.1.call-start = ((), (), s32[]{:S(2)}) async-start(), calls=%async_computation.6 | async-start | bytes 7864320 | tf_op jit(solution)/shard_map/all_gather | solution.py:84
  10.0 73.5 %all-gather.23.cloned.1.call-start = ((), (), s32[]{:S(2)}) async-start(), calls=%async_computation.8 | async-start | bytes 2621440 | tf_op jit(solution)/shard_map/all_gather | solution.py:85
  10.8 96.1 %all-gather.21.cloned.1.call-start = ((), (), s32[]{:S(2)}) async-start(), calls=%async_computation.7 | async-start | bytes 1572864 | tf_op jit(solution)/shard_map/all_gather | solution.py:132
  11.0 12.1 copy-start.26
  17.2 48.0 %copy-start.28 = (f32[4,1,512]{2,1,0:T(1,128)}, f32[4,1,512]{2,1,0:T(1,128)S(1)}, u32[]{:S(2)}) copy-start(f32[4,1,512]{2,1,0:T(1,128)S(1)} %convert_element_type.153) | copy-start | bytes 24580
  23.0 45.6 %copy-start.27 = (s32[512]{0:T(512)}, s32[512]{0:T(512)S(1)}, u32[]{:S(2)}) copy-start(s32[512]{0:T(512)S(1)} %get-tuple-element.65) | copy-start | bytes 6148
  24.5 41.1 %copy-start.21 = (f32[512,32]{0,1:T(8,128)}, f32[512,32]{0,1:T(8,128)S(1)}, u32[]{:S(2)}) copy-start(f32[512,32]{0,1:T(8,128)S(1)} %get-tuple-element.92) | copy-start | bytes 196612
  24.5 41.1 %copy-start.22 = (f32[512,32]{0,1:T(8,128)}, f32[512,32]{0,1:T(8,128)S(1)}, u32[]{:S(2)}) copy-start(f32[512,32]{0,1:T(8,128)S(1)} %get-tuple-element.93) | copy-start | bytes 196612
  67.8 62.4 %all-gather.37.cloned.1.call-start = ((), (), s32[]{:S(2)}) async-start(), calls=%async_computation.21 | async-start | bytes 1572864 | tf_op jit(solution)/shard_map/all_gather | solution.py:133
  68.0 19.8 %copy-start.25 = (s32[1024]{0:T(1024)}, s32[1024]{0:T(1024)S(1)}, u32[]{:S(2)}) copy-start(s32[1024]{0:T(1024)S(1)} %fusion.79) | copy-start | bytes 12292
  90.0 74.9 %reduce-scatter.9.cloned.1.call-start = ((), (), s32[]{:S(2)}) async-start(), calls=%async_computation.12 | async-start | bytes 3145728 | tf_op jit(solution)/shard_map/reduce_scatter | solution.py:215
  114.3 85.2 %reduce-scatter.7.cloned.1.call-start = ((), (), s32[]{:S(2)}) async-start(), calls=%async_computation.11 | async-start | bytes 3145728 | tf_op jit(solution)/shard_map/reduce_scatter | solution.py:214
  138.6 120.8 %all-gather.25.cloned.1.call-start = ((), (), s32[]{:S(2)}) async-start(), calls=%async_computation.9 | async-start | bytes 10485760 | tf_op jit(solution)/shard_map/all_gather | solution.py:86
  139.3 179.9 %all-gather.27.cloned.1.call-start = ((), (), s32[]{:S(2)}) async-start(), calls=%async_computation.10 | async-start | bytes 10485760 | tf_op jit(solution)/shard_map/all_gather | solution.py:87
  140.1 234.2 %reduce-scatter.13.cloned.1.call-start = ((), (), s32[]{:S(2)}) async-start(), calls=%async_computation.15 | async-start | bytes 4718592 | tf_op jit(solution)/shard_map/reduce_scatter | solution.py:241
  147.5 322.2 %reduce-scatter.11.cloned.1.call-start = ((), (), s32[]{:S(2)}) async-start(), calls=%async_computation.13 | async-start | bytes 14155776 | tf_op jit(solution)/shard_map/reduce_scatter | solution.py:240
  216.0 43.3 %copy-start.29 = (f32[4,1,512]{2,1,0:T(1,128)S(1)}, f32[4,1,512]{2,1,0:T(1,128)}, u32[]{:S(2)}) copy-start(f32[4,1,512]{2,1,0:T(1,128)} %copy-done.28) | copy-start | bytes 24580
  216.0 373.4 %reduce-scatter.15.cloned.1.call-start = ((), (), s32[]{:S(2)}) async-start(), calls=%async_computation.17 | async-start | bytes 18874368 | tf_op jit(solution)/shard_map/reduce_scatter | solution.py:242
  338.7 370.2 %reduce-scatter.17.cloned.1.call-start = ((), (), s32[]{:S(2)}) async-start(), calls=%async_computation.19 | async-start | bytes 18874368 | tf_op jit(solution)/shard_map/reduce_scatter | solution.py:243
  351.8 380.0 %all-gather.31.cloned.1.call-start = ((), (), s32[]{:S(2)}) async-start(), calls=%async_computation.16 | async-start | bytes 1572864 | tf_op jit(solution)/shard_map/all_gather | solution.py:250
  353.3 10.8 copy-start.42
  374.3 6.7 copy-start.14
  374.3 651.4 %all-reduce.7.cloned.1.call-start = ((), (), s32[]{:S(2)}) async-start(), calls=%async_computation.22 | async-start | bytes 16777216 | tf_op jit(solution)/shard_map/psum | solution.py:172
  389.7 319.2 %copy-start.35 = (bf16[512]{0:T(512)(128)(2,1)S(1)}, bf16[512]{0:T(512)(128)(2,1)}, u32[]{:S(2)}) copy-start(bf16[512]{0:T(512)(128)(2,1)} %param.22) | copy-start | bytes 3076
  389.8 319.2 %copy-start.36 = (bf16[512]{0:T(512)(128)(2,1)S(1)}, bf16[512]{0:T(512)(128)(2,1)}, u32[]{:S(2)}) copy-start(bf16[512]{0:T(512)(128)(2,1)} %param.26) | copy-start | bytes 3076
  389.8 319.2 %copy-start.39 = (u32[32]{0:T(128)S(1)}, u32[32]{0:T(128)}, u32[]{:S(2)}) copy-start(u32[32]{0:T(128)} %constant.160) | copy-start | bytes 388
  389.8 687.7 %all-gather.29.cloned.1.call-start = ((), (), s32[]{:S(2)}) async-start(), calls=%async_computation.14 | async-start | bytes 4718592 | tf_op jit(solution)/shard_map/all_gather | solution.py:249
  469.7 661.9 %all-gather.33.cloned.1.call-start = ((), (), s32[]{:S(2)}) async-start(), calls=%async_computation.18 | async-start | bytes 6291456 | tf_op jit(solution)/shard_map/all_gather | solution.py:251
  589.5 600.3 %all-gather.35.cloned.1.call-start = ((), (), s32[]{:S(2)}) async-start(), calls=%async_computation.20 | async-start | bytes 6291456 | tf_op jit(solution)/shard_map/all_gather | solution.py:252
  (28 other events, 78.8 us)
Sparse Core Ops, SparseCore 0:
  10.2 49.1 all-gather.18
  60.9 22.5 all-gather.22
  85.6 21.2 all-gather.20
  108.9 21.2 all-gather.36
  132.9 31.9 reduce-scatter.8
  167.5 31.8 reduce-scatter.6
  201.0 58.2 all-gather.24
  260.9 58.2 all-gather.26
  323.1 51.0 reduce-scatter.12
  377.6 92.0 reduce-scatter.10
  473.2 116.1 reduce-scatter.14
  592.9 115.9 reduce-scatter.16
  710.4 21.2 all-gather.30
  734.8 290.8 all-reduce.6
  1027.0 46.3 all-gather.28
  1074.9 56.7 all-gather.32
  1133.0 56.7 all-gather.34
where the time goes:
time: 1220 us; the launch traced here: 1210 us
  waiting for transfers between devices  942 us (77%)
  matrix products  122 us (10%)
  blocking collectives  63.4 us (5%)
  local copies, waits for them, and re-layouts  37.8 us (3%)
  other arithmetic  27.6 us (2%)
  between operations  15.6 us (1%)
    psum x1, waiting for transfers between devices, per_device(): summed = lax.psum(partial_out, 'tp')  291 us
    reduce_scatter x1, waiting for transfers between devices, per_device(): lax.psum_scatter(fc1_grad, ('fsdp', 'ctx'), scatter_dimension=0, tiled=True)  120 us
    reduce_scatter x1, waiting for transfers between devices, per_device(): lax.psum_scatter(fc2_grad, ('fsdp', 'ctx'), scatter_dimension=0, tiled=True)  119 us
    reduce_scatter x1, waiting for transfers between devices, per_device(): lax.psum_scatter(qkv_grad, ('fsdp', 'ctx'), scatter_dimension=0, tiled=True)  79.9 us
    all_gather x1, waiting for transfers between devices, per_device(): lax.all_gather(reduced[3], 'ctx', axis=0, tiled=True)  58.1 us
    all_gather x1, waiting for transfers between devices, per_device(): lax.all_gather(reduced[2], 'ctx', axis=0, tiled=True)  54.2 us
    all_gather x1, waiting for transfers between devices, per_device(): lax.all_gather(fc2_weight, 'fsdp', axis=0, tiled=True)  42.7 us
    all_gather x1, waiting for transfers between devices, per_device(): lax.all_gather(fc1_weight, 'fsdp', axis=0, tiled=True)  42.6 us
  transfers between devices with their start and end apart: 17, of which 16 were waited for; matrix products, arithmetic and copies ran while one was open for 14% of the time, Pallas kernels for 0%

commit v1 on v0

--- a/solution.py
+++ b/solution.py
@@ -169,7 +169,7 @@
     partial_out = jnp.einsum(
         "te,de->td", attended, dense_full, preferred_element_type=jnp.float32
     ) + jnp.einsum("tf,df->td", hidden, fc2_full, preferred_element_type=jnp.float32)
-    summed = lax.psum(partial_out, "tp")
+    summed = jnp.sum(lax.all_gather(partial_out, "tp"), axis=0)
     output = (inputs + summed + out_bias).astype(jnp.bfloat16)
     upstream_low = cotangent[0]
     upstream = upstream_low.astype(jnp.float32)

time: 1220 us -> 1370 us (1.12)
  waiting for transfers between devices: 942 us -> 1090 us
    all_gather x0 -> x1, waiting for transfers between devices: none -> 287 us  [per_device(): summed = jnp.sum(lax.all_gather(partial_out, 'tp'), axis=0)]
    psum x1, waiting for transfers between devices: 291 us -> 155 us  [per_device(): full_grad = lax.psum(normed_grad, 'tp')]
    reduce_scatter x1, waiting for transfers between devices: 0.33 us -> 22.4 us  [per_device(): lax.psum_scatter(dense_grad, ('fsdp', 'ctx'), scatter_dimension=0, tiled=...]
  transfers between devices with their start and end apart: 17 -> 18, of which waited for: 16 -> 17; matrix products, arithmetic and copies ran while one was open for 14% -> 12% of each run, Pallas kernels for 0% -> 0%
where the time goes in v1:
time: 1370 us; the launch traced here: 1360 us
  waiting for transfers between devices  1090 us (80%)
  matrix products  114 us (8%)
  blocking collectives  63.7 us (5%)
  other arithmetic  38.9 us (3%)
  local copies, waits for them, and re-layouts  37.2 us (3%)
  between operations  16 us (1%)
    all_gather x1, waiting for transfers between devices, per_device(): summed = jnp.sum(lax.all_gather(partial_out, 'tp'), axis=0)  287 us
    psum x1, waiting for transfers between devices, per_device(): full_grad = lax.psum(normed_grad, 'tp')  155 us
    reduce_scatter x1, waiting for transfers between devices, per_device(): lax.psum_scatter(fc2_grad, ('fsdp', 'ctx'), scatter_dimension=0, tiled=True)  119 us
    reduce_scatter x1, waiting for transfers between devices, per_device(): lax.psum_scatter(fc1_grad, ('fsdp', 'ctx'), scatter_dimension=0, tiled=True)  108 us
    reduce_scatter x1, waiting for transfers between devices, per_device(): lax.psum_scatter(qkv_grad, ('fsdp', 'ctx'), scatter_dimension=0, tiled=True)  78.6 us
    all_gather x1, waiting for transfers between devices, per_device(): lax.all_gather(reduced[3], 'ctx', axis=0, tiled=True)  58.2 us
    all_gather x1, waiting for transfers between devices, per_device(): lax.all_gather(fc2_weight, 'fsdp', axis=0, tiled=True)  42.6 us
    all_gather x1, waiting for transfers between devices, per_device(): lax.all_gather(fc1_weight, 'fsdp', axis=0, tiled=True)  42.6 us
  transfers between devices with their start and end apart: 18, of which 17 were waited for; matrix products, arithmetic and copies ran while one was open for 12% of the time, Pallas kernels for 0%

profile of v1, /device:TPU:0, one launch (start us, length us, event | category | flops | bytes accessed | tf_op | source)
XLA Modules:
  0.0 1361.0 jit_solution(3118643967423950156)
XLA Ops:
  11.0 6.2 all-gather.3
  17.2 5.5 all-gather.2
  24.5 34.9 %all-gather.21.cloned.1.call-done = bf16[2048,3,512]{0,2,1:T(8,128)(2,1)} async-done(((bf16[512,3,512]{0,2,1:T(8,128)(2,1)}), bf16[2048,3,512]{0,2,1:T(8,128)(2,1)}) %all-gather.21.cloned.1.call-update) | async-done | bytes 6291472 | tf_op jit(solution)/shard_map/all_gather | solution.py:84
  59.3 5.9 fusion.44
  68.7 14.8 %all-gather.25.cloned.1.call-done = bf16[2048,512]{1,0:T(8,128)(2,1)} async-done(((bf16[512,512]{1,0:T(8,128)(2,1)}), bf16[2048,512]{1,0:T(8,128)(2,1)}) %all-gather.25.cloned.1.call-update) | async-done | bytes 2097168 | tf_op jit(solution)/shard_map/all_gather | solution.py:85
  90.9 16.0 %all-gather.23.cloned.1.call-done = bf16[1024,2,256]{0,2,1:T(8,128)(2,1)} async-done(((bf16[512,2,256]{0,2,1:T(8,128)(2,1)}), bf16[1024,2,256]{0,2,1:T(8,128)(2,1)}) %all-gather.23.cloned.1.call-update) | async-done | bytes 1048592 | tf_op jit(solution)/shard_map/all_gather | solution.py:132
  114.5 15.7 %all-gather.39.cloned.1.call-done = bf16[1024,1,2,256]{0,3,2,1:T(8,128)(2,1)} async-done(((bf16[512,1,2,256]{0,3,2,1:T(8,128)(2,1)}), bf16[1024,1,2,256]{0,3,2,1:T(8,128)(2,1)}) %all-gather.39.cloned.1.call-update) | async-done | bytes 1048592 | tf_op jit(solution)/shard_map/all_gather | solution.py:133
  152.3 12.6 reduce-scatter.9.cloned.1.call-done
  171.0 28.5 %reduce-scatter.7.cloned.1.call-done = f32[512,2,256]{0,2,1:T(8,128)} async-done(((f32[1024,2,256]{0,2,1:T(8,128)}), f32[512,2,256]{0,2,1:T(8,128)}) %reduce-scatter.7.cloned.1.call-update) | async-done | bytes 1048592 | tf_op jit(solution)/shard_map/reduce_scatter | solution.py:214
  207.2 8.9 fusion.38
  216.7 42.6 %all-gather.27.cloned.1.call-done = bf16[2048,2048]{1,0:T(8,128)(2,1)} async-done(((bf16[512,2048]{1,0:T(8,128)(2,1)}), bf16[2048,2048]{1,0:T(8,128)(2,1)}) %all-gather.27.cloned.1.call-update) | async-done | bytes 8388624 | tf_op jit(solution)/shard_map/all_gather | solution.py:86
  259.3 17.2 %fusion.19 = (bf16[512,2048]{1,0:T(8,128)(2,1)}, f32[512,2048]{1,0:T(8,128)}) fusion(f32[2048]{0:T(1024)S(1)} %convert_element_type.137, bf16[2048,2048]{1,0:T(8,128)(2,1)} %all-gather.27.cloned.1.call-done, bf16[1,512,2048]{2,1,0:T(8,128)(2,1)S(1)} %copy-done, f32[2048]{0:T(1024)S(1)} %bitcast.215, f32[2048]{0:T(1024)S(1)} %bitcast.206, ...), kind=kOutput, calls=%fused_computation.27 | convolution fusion | flops 4370464768 | bytes 16805888 | tf_op jit(solution)/shard_map/dot_general | solution.py:165
  276.5 42.6 %all-gather.29.cloned.1.call-done = bf16[2048,2048]{1,0:T(8,128)(2,1)} async-done(((bf16[512,2048]{1,0:T(8,128)(2,1)}), bf16[2048,2048]{1,0:T(8,128)(2,1)}) %all-gather.29.cloned.1.call-update) | async-done | bytes 8388624 | tf_op jit(solution)/shard_map/all_gather | solution.py:87
  319.2 9.4 convert_reduce_fusion.2
  329.9 8.8 fusion.90
  339.2 12.5 convolution_bitcast_fusion
  351.8 22.4 %reduce-scatter.13.cloned.1.call-done = f32[256,512]{0,1:T(8,128)} async-done(((f32[2048,512]{0,1:T(8,128)}), f32[256,512]{0,1:T(8,128)}) %reduce-scatter.13.cloned.1.call-update) | async-done | bytes 524304 | tf_op jit(solution)/shard_map/reduce_scatter | solution.py:241
  374.3 7.7 fusion.98
  382.1 8.8 bitcast_add_fusion
  391.0 78.6 %reduce-scatter.11.cloned.1.call-done = f32[256,3,512]{2,0,1:T(8,128)} async-done(((f32[2048,3,512]{2,0,1:T(8,128)}), f32[256,3,512]{2,0,1:T(8,128)}) %reduce-scatter.11.cloned.1.call-update) | async-done | bytes 1572880 | tf_op jit(solution)/shard_map/reduce_scatter | solution.py:240
  469.9 7.8 fusion.97
  481.1 108.4 %reduce-scatter.15.cloned.1.call-done = f32[256,2048]{1,0:T(8,128)} async-done(((f32[2048,2048]{1,0:T(8,128)}), f32[256,2048]{1,0:T(8,128)}) %reduce-scatter.15.cloned.1.call-update) | async-done | bytes 2097168 | tf_op jit(solution)/shard_map/reduce_scatter | solution.py:242
  589.5 119.4 %reduce-scatter.17.cloned.1.call-done = f32[256,2048]{0,1:T(8,128)} async-done(((f32[2048,2048]{0,1:T(8,128)}), f32[256,2048]{0,1:T(8,128)}) %reduce-scatter.17.cloned.1.call-update) | async-done | bytes 2097168 | tf_op jit(solution)/shard_map/reduce_scatter | solution.py:243
  715.4 5.3 all-gather.4
  722.1 9.7 all-gather.33.cloned.1.call-done
  734.3 155.3 %all-reduce.6.cloned.1.call-done = f32[512,2048]{1,0:T(8,128)} async-done(((f32[512,2048]{1,0:T(8,128)}), f32[512,2048]{1,0:T(8,128)}) %all-reduce.6.cloned.1.call-update) | async-done | bytes 4194320 | tf_op jit(solution)/shard_map/psum | solution.py:229
  897.3 28.5 %all-reduce.3 = (f32[2048]{0:T(1024)S(1)}, f32[2048]{0:T(1024)S(1)}, f32[3,512]{1,0:T(4,128)}, f32[2048]{0:T(1024)S(1)}, f32[2048]{0:T(1024)}) all-reduce(f32[2048]{0:T(1024)S(1)} %get-tuple-element.60, f32[2048]{0:T(1024)S(1)} %get-tuple-element.63, ...), channel_id=6, replica_groups=mesh['fsdp'=4,'ctx'=2,'tp'=4] {'fsdp','ctx'}, use_global_device_ids=true, to_apply=%region_21.22.clone | all-reduce | flops 9728 | bytes 77824
  939.0 286.9 %all-gather.41.cloned.1.call-done = f32[2048,2048]{1,0:T(8,128)} async-done(((f32[512,2048]{1,0:T(8,128)}), f32[2048,2048]{1,0:T(8,128)}) %all-gather.41.cloned.1.call-update) | async-done | bytes 16777232 | tf_op jit(solution)/shard_map/all_gather | solution.py:172
  1226.0 10.5 reduce_sum.182
  1241.1 41.2 %all-gather.35.cloned.1.call-done = f32[512,2048]{1,0:T(8,128)} async-done(((f32[256,2048]{1,0:T(8,128)}), f32[512,2048]{1,0:T(8,128)}) %all-gather.35.cloned.1.call-update) | async-done | bytes 4194320 | tf_op jit(solution)/shard_map/all_gather | solution.py:251
  1282.3 58.2 %all-gather.37.cloned.1.call-done = f32[512,2048]{0,1:T(8,128)} async-done(((f32[256,2048]{0,1:T(8,128)}), f32[512,2048]{0,1:T(8,128)}) %all-gather.37.cloned.1.call-update) | async-done | bytes 4194320 | tf_op jit(solution)/shard_map/all_gather | solution.py:252
  1340.5 5.3 copy.67
  (214 shorter events, 109.0 us)
Async XLA Ops:
  7.2 15.8 %copy-start = (bf16[1,512,2048]{2,1,0:T(8,128)(2,1)S(1)}, bf16[1,512,2048]{2,1,0:T(8,128)(2,1)}, u32[]{:S(2)}) copy-start(bf16[1,512,2048]{2,1,0:T(8,128)(2,1)} %param.14) | copy-start | bytes 6291460
  7.2 52.1 %all-gather.21.cloned.1.call-start = ((), (), s32[]{:S(2)}) async-start(), calls=%async_computation.6 | async-start | bytes 7864320 | tf_op jit(solution)/shard_map/all_gather | solution.py:84
  10.0 73.5 %all-gather.25.cloned.1.call-start = ((), (), s32[]{:S(2)}) async-start(), calls=%async_computation.8 | async-start | bytes 2621440 | tf_op jit(solution)/shard_map/all_gather | solution.py:85
  10.8 96.1 %all-gather.23.cloned.1.call-start = ((), (), s32[]{:S(2)}) async-start(), calls=%async_computation.7 | async-start | bytes 1572864 | tf_op jit(solution)/shard_map/all_gather | solution.py:132
  17.2 48.0 %copy-start.31 = (f32[4,1,512]{2,1,0:T(1,128)}, f32[4,1,512]{2,1,0:T(1,128)S(1)}, u32[]{:S(2)}) copy-start(f32[4,1,512]{2,1,0:T(1,128)S(1)} %convert_element_type.155) | copy-start | bytes 24580
  23.0 45.6 %copy-start.30 = (s32[512]{0:T(512)}, s32[512]{0:T(512)S(1)}, u32[]{:S(2)}) copy-start(s32[512]{0:T(512)S(1)} %get-tuple-element.65) | copy-start | bytes 6148
  24.1 41.1 %copy-start.26 = (f32[512]{0:T(512)}, f32[512]{0:T(512)S(1)}, u32[]{:S(2)}) copy-start(f32[512]{0:T(512)S(1)} %add_rsqrt_fusion) | copy-start | bytes 6148
  24.5 41.1 %copy-start.24 = (f32[512,32]{0,1:T(8,128)}, f32[512,32]{0,1:T(8,128)S(1)}, u32[]{:S(2)}) copy-start(f32[512,32]{0,1:T(8,128)S(1)} %get-tuple-element.89) | copy-start | bytes 196612
  24.5 41.1 %copy-start.25 = (f32[512,32]{0,1:T(8,128)}, f32[512,32]{0,1:T(8,128)S(1)}, u32[]{:S(2)}) copy-start(f32[512,32]{0,1:T(8,128)S(1)} %get-tuple-element.90) | copy-start | bytes 196612
  67.8 62.4 %all-gather.39.cloned.1.call-start = ((), (), s32[]{:S(2)}) async-start(), calls=%async_computation.22 | async-start | bytes 1572864 | tf_op jit(solution)/shard_map/all_gather | solution.py:133
  68.0 19.8 %copy-start.28 = (s32[1024]{0:T(1024)}, s32[1024]{0:T(1024)S(1)}, u32[]{:S(2)}) copy-start(s32[1024]{0:T(1024)S(1)} %fusion.77) | copy-start | bytes 12292
  90.0 74.9 %reduce-scatter.9.cloned.1.call-start = ((), (), s32[]{:S(2)}) async-start(), calls=%async_computation.12 | async-start | bytes 3145728 | tf_op jit(solution)/shard_map/reduce_scatter | solution.py:215
  114.3 85.2 %reduce-scatter.7.cloned.1.call-start = ((), (), s32[]{:S(2)}) async-start(), calls=%async_computation.11 | async-start | bytes 3145728 | tf_op jit(solution)/shard_map/reduce_scatter | solution.py:214
  138.6 120.8 %all-gather.27.cloned.1.call-start = ((), (), s32[]{:S(2)}) async-start(), calls=%async_computation.9 | async-start | bytes 10485760 | tf_op jit(solution)/shard_map/all_gather | solution.py:86
  139.3 179.9 %all-gather.29.cloned.1.call-start = ((), (), s32[]{:S(2)}) async-start(), calls=%async_computation.10 | async-start | bytes 10485760 | tf_op jit(solution)/shard_map/all_gather | solution.py:87
  140.1 234.2 %reduce-scatter.13.cloned.1.call-start = ((), (), s32[]{:S(2)}) async-start(), calls=%async_computation.16 | async-start | bytes 4718592 | tf_op jit(solution)/shard_map/reduce_scatter | solution.py:241
  147.4 322.2 %reduce-scatter.11.cloned.1.call-start = ((), (), s32[]{:S(2)}) async-start(), calls=%async_computation.14 | async-start | bytes 14155776 | tf_op jit(solution)/shard_map/reduce_scatter | solution.py:240
  216.0 43.3 %copy-start.27 = (f32[512]{0:T(512)S(1)}, f32[512]{0:T(512)}, u32[]{:S(2)}) copy-start(f32[512]{0:T(512)} %copy-done.26) | copy-start | bytes 6148
  216.0 43.3 %copy-start.32 = (f32[4,1,512]{2,1,0:T(1,128)S(1)}, f32[4,1,512]{2,1,0:T(1,128)}, u32[]{:S(2)}) copy-start(f32[4,1,512]{2,1,0:T(1,128)} %copy-done.31) | copy-start | bytes 24580
  216.1 373.4 %reduce-scatter.15.cloned.1.call-start = ((), (), s32[]{:S(2)}) async-start(), calls=%async_computation.18 | async-start | bytes 18874368 | tf_op jit(solution)/shard_map/reduce_scatter | solution.py:242
  338.7 370.1 %reduce-scatter.17.cloned.1.call-start = ((), (), s32[]{:S(2)}) async-start(), calls=%async_computation.20 | async-start | bytes 18874368 | tf_op jit(solution)/shard_map/reduce_scatter | solution.py:243
  351.8 380.0 %all-gather.33.cloned.1.call-start = ((), (), s32[]{:S(2)}) async-start(), calls=%async_computation.17 | async-start | bytes 1572864 | tf_op jit(solution)/shard_map/all_gather | solution.py:250
  374.3 515.3 %all-reduce.6.cloned.1.call-start = ((), (), s32[]{:S(2)}) async-start(), calls=%async_computation.13 | async-start | bytes 8388608 | tf_op jit(solution)/shard_map/psum | solution.py:229
  391.0 548.1 %all-gather.31.cloned.1.call-start = ((), (), s32[]{:S(2)}) async-start(), calls=%async_computation.15 | async-start | bytes 4718592 | tf_op jit(solution)/shard_map/all_gather | solution.py:249
  469.7 756.3 %all-gather.41.cloned.1.call-start = ((), (), s32[]{:S(2)}) async-start(), calls=%async_computation.23 | async-start | bytes 20971520 | tf_op jit(solution)/shard_map/all_gather | solution.py:172
  481.0 227.9 %copy-start.38 = (bf16[512]{0:T(512)(128)(2,1)S(1)}, bf16[512]{0:T(512)(128)(2,1)}, u32[]{:S(2)}) copy-start(bf16[512]{0:T(512)(128)(2,1)} %param.22) | copy-start | bytes 3076
  481.0 228.0 %copy-start.39 = (bf16[512]{0:T(512)(128)(2,1)S(1)}, bf16[512]{0:T(512)(128)(2,1)}, u32[]{:S(2)}) copy-start(bf16[512]{0:T(512)(128)(2,1)} %param.26) | copy-start | bytes 3076
  481.0 228.0 %copy-start.42 = (u32[32]{0:T(128)S(1)}, u32[32]{0:T(128)}, u32[]{:S(2)}) copy-start(u32[32]{0:T(128)} %constant.160) | copy-start | bytes 388
  481.0 239.8 %copy-start.15 = (bf16[512,1,512]{2,0,1:T(8,128)(2,1)S(1)}, bf16[512,1,512]{2,0,1:T(8,128)(2,1)}, u32[]{:S(2)}) copy-start(bf16[512,1,512]{2,0,1:T(8,128)(2,1)} %copy.63) | copy-start | bytes 1572868
  481.0 239.8 %copy-start.17 = (bf16[512,1,512]{2,0,1:T(8,128)(2,1)S(1)}, bf16[512,1,512]{2,0,1:T(8,128)(2,1)}, u32[]{:S(2)}) copy-start(bf16[512,1,512]{2,0,1:T(8,128)(2,1)} %copy.61) | copy-start | bytes 1572868
  481.0 801.3 %all-gather.35.cloned.1.call-start = ((), (), s32[]{:S(2)}) async-start(), calls=%async_computation.19 | async-start | bytes 6291456 | tf_op jit(solution)/shard_map/all_gather | solution.py:251
  589.5 751.0 %all-gather.37.cloned.1.call-start = ((), (), s32[]{:S(2)}) async-start(), calls=%async_computation.21 | async-start | bytes 6291456 | tf_op jit(solution)/shard_map/all_gather | solution.py:252
  (30 other events, 131.9 us)
Sparse Core Ops, SparseCore 0:
  10.2 49.1 all-gather.20
  60.9 22.5 all-gather.24
  85.6 21.2 all-gather.22
  108.9 21.2 all-gather.38
  132.9 31.9 reduce-scatter.8
  167.5 31.8 reduce-scatter.6
  201.0 58.2 all-gather.26
  260.9 58.2 all-gather.28
  323.1 51.0 reduce-scatter.12
  377.6 92.0 reduce-scatter.10
  473.2 116.1 reduce-scatter.14
  592.9 115.9 reduce-scatter.16
  710.4 21.2 all-gather.32
  734.5 154.9 all-reduce.5
  890.9 46.3 all-gather.30
  939.3 286.5 all-gather.40
  1227.4 54.8 all-gather.34
  1283.7 56.7 all-gather.36
